TPU v7x, 128 devices: a whole 4x4x4 slice. The times are simulated.
128 devices in a mesh: row: 8 (over y, z_hi), col: 16 (over z_lo, x, core).
Axes of the slice: x: 4, y: 4, z: 4 (z_hi: 2, z_lo: 2; z = z_hi * 2 + z_lo), core: 2. Of those that a mesh axis runs over, the one named last changes fastest.
Arguments:
- features: float32 [2, 128, 1024, 128], P(None, 'row', 'col'), may hold values from -6 to 6
- cotangent: float32 [2, 128, 1024, 128], P(None, 'row', 'col'), may hold values from -6 to 6
- conv_kernel: float32 [7, 7, 128], P(None, None, ('row', 'col')), may hold values from -0.875 to 0.875
- conv_bias: float32 [128], P(('row', 'col')), may hold values from -3 to 3
- norm_gain: float32 [128], P(('row', 'col')), may hold values from 0.1 to 1.9
- norm_shift: float32 [128], P(('row', 'col')), may hold values from -2 to 2
- w_in: float32 [128, 512], P(None, ('row', 'col')), may hold values from -0.5 to 0.5
- in_bias: float32 [512], P(('row', 'col')), may hold values from -3 to 3
- w_out: float32 [512, 128], P(('row', 'col')), may hold values from -0.25 to 0.25
- out_bias: float32 [128], P(('row', 'col')), may hold values from -3 to 3
- layer_scale: float32 [128], P(('row', 'col')), may hold values from 0.5 to 1.5
Outputs:
- features_grad: float32 [2, 128, 1024, 128], P(None, 'row', 'col')
- kernel_grad: float32 [7, 7, 128], P(None, None, ('row', 'col'))
- conv_bias_grad: float32 [128], P(('row', 'col'))
- gain_grad: float32 [128], P(('row', 'col'))
- shift_grad: float32 [128], P(('row', 'col'))
- w_in_grad: float32 [128, 512], P(None, ('row', 'col'))
- in_bias_grad: float32 [512], P(('row', 'col'))
- w_out_grad: float32 [512, 128], P(('row', 'col'))
- out_bias_grad: float32 [128], P(('row', 'col'))
- scale_grad: float32 [128], P(('row', 'col'))
All inputs are finite; a program needn't handle non-finite values.
Results may differ from a plain program's by a relative error of at most 0.0003.
Values sent between devices are 32-bit elements; how exact they have to be, the bound alone decides.
A program may use at most 64 MiB of HBM per device.

v0:
```python
import math
import jax
import jax.numpy as jnp
from jax import lax
from jax.sharding import PartitionSpec as P

norm_eps = 1e-06
inverse_root_two = 0.7071067811865476
inverse_root_twopi = 0.3989422804014327


def extended(block, sides, width):
    for axis, dim in sides:
        count = lax.axis_size(axis)
        forward = [(i, i + 1) for i in range(count - 1)]
        backward = [(target, source) for source, target in forward]
        low = lax.ppermute(
            lax.slice_in_dim(block, block.shape[dim] - width, None, axis=dim), axis, forward
        )
        high = lax.ppermute(lax.slice_in_dim(block, 0, width, axis=dim), axis, backward)
        block = jnp.concatenate([low, block, high], axis=dim)
    return block


def depthwise(field, kernel):
    return lax.conv_general_dilated(
        field,
        kernel[:, :, None, :],
        (1, 1),
        "VALID",
        dimension_numbers=("NHWC", "HWIO", "NHWC"),
        feature_group_count=field.shape[-1],
        precision=lax.Precision.HIGHEST,
    )


def cell_total(block):
    return jnp.sum(block, axis=(0, 1, 2))


def mixing_back(
    conv_out,
    cot_field,
    gain_all,
    shift_all,
    input_all,
    inbias_all,
    output_all,
    outbias_all,
    scale_all,
):
    highest = lax.Precision.HIGHEST
    mean = jnp.mean(conv_out, -1, keepdims=True)
    centred = conv_out - mean
    variance = jnp.mean(centred * centred, -1, keepdims=True)
    inverse = lax.rsqrt(variance + norm_eps)
    normed = centred * inverse
    lin = normed * gain_all + shift_all
    act = jnp.einsum("bhwc,ck->bhwk", lin, input_all, precision=highest) + inbias_all
    hidden = 0.5 * act * (1.0 + lax.erf(act * inverse_root_two))
    branch = jnp.einsum("bhwk,kc->bhwc", hidden, output_all, precision=highest) + outbias_all
    d_branch = cot_field * scale_all
    d_hidden = jnp.einsum("bhwc,kc->bhwk", d_branch, output_all, precision=highest)
    slope = (
        0.5 * (1.0 + lax.erf(act * inverse_root_two))
        + act * jnp.exp(-0.5 * act * act) * inverse_root_twopi
    )
    d_act = d_hidden * slope
    d_lin = jnp.einsum("bhwk,ck->bhwc", d_act, input_all, precision=highest)
    d_norm = d_lin * gain_all
    d_conv = inverse * (
        d_norm
        - jnp.mean(d_norm, -1, keepdims=True)
        - normed * jnp.mean(d_norm * normed, -1, keepdims=True)
    )
    gain_grad = cell_total(d_lin * normed)
    shift_grad = cell_total(d_lin)
    win_grad = jnp.einsum("bhwc,bhwk->ck", lin, d_act, precision=highest)
    inb_grad = cell_total(d_act)
    wout_grad = jnp.einsum("bhwk,bhwc->kc", hidden, d_branch, precision=highest)
    outb_grad = cell_total(d_branch)
    scale_grad = cell_total(cot_field * branch)
    return (d_conv, (gain_grad, shift_grad, win_grad, inb_grad, wout_grad, outb_grad, scale_grad))


def per_device(
    features,
    cotangent,
    conv_kernel,
    conv_bias,
    norm_gain,
    norm_shift,
    w_in,
    in_bias,
    w_out,
    out_bias,
    layer_scale,
):
    gathered = (
        lax.all_gather(conv_kernel, ("row", "col"), axis=2, tiled=True),
        lax.all_gather(conv_bias, ("row", "col"), axis=0, tiled=True),
        lax.all_gather(norm_gain, ("row", "col"), axis=0, tiled=True),
        lax.all_gather(norm_shift, ("row", "col"), axis=0, tiled=True),
        lax.all_gather(w_in, ("row", "col"), axis=1, tiled=True),
        lax.all_gather(in_bias, ("row", "col"), axis=0, tiled=True),
        lax.all_gather(w_out, ("row", "col"), axis=0, tiled=True),
        lax.all_gather(out_bias, ("row", "col"), axis=0, tiled=True),
        lax.all_gather(layer_scale, ("row", "col"), axis=0, tiled=True),
    )
    (
        kernel_all,
        conv_all,
        gain_all,
        shift_all,
        input_all,
        inbias_all,
        output_all,
        outbias_all,
        scale_all,
    ) = gathered
    margin = kernel_all.shape[0] // 2
    source = extended(features, (("row", 1), ("col", 2)), margin)
    conv_out = depthwise(source, kernel_all) + conv_all
    dconv_inner, partials = mixing_back(
        conv_out,
        cotangent,
        gain_all,
        shift_all,
        input_all,
        inbias_all,
        output_all,
        outbias_all,
        scale_all,
    )
    dconv_wide = extended(dconv_inner, (("row", 1), ("col", 2)), margin)
    features_grad = cotangent + depthwise(dconv_wide, kernel_all[::-1, ::-1])
    kernel_part = jax.vjp(lambda weights: depthwise(source, weights), kernel_all)[1](dconv_inner)[0]
    bias_part = jnp.sum(dconv_inner, axis=(0, 1, 2))
    cells = (
        features.shape[0]
        * features.shape[1]
        * features.shape[2]
        * lax.axis_size("row")
        * lax.axis_size("col")
    )
    factor = 1.0 / math.sqrt(cells)
    gain_p, shift_p, win_p, inb_p, wout_p, outb_p, scale_p = partials
    reduced = (
        lax.psum_scatter(kernel_part * factor, ("row", "col"), scatter_dimension=2, tiled=True),
        lax.psum_scatter(bias_part * factor, ("row", "col"), scatter_dimension=0, tiled=True),
        lax.psum_scatter(gain_p * factor, ("row", "col"), scatter_dimension=0, tiled=True),
        lax.psum_scatter(shift_p * factor, ("row", "col"), scatter_dimension=0, tiled=True),
        lax.psum_scatter(win_p * factor, ("row", "col"), scatter_dimension=1, tiled=True),
        lax.psum_scatter(inb_p * factor, ("row", "col"), scatter_dimension=0, tiled=True),
        lax.psum_scatter(wout_p * factor, ("row", "col"), scatter_dimension=0, tiled=True),
        lax.psum_scatter(outb_p * factor, ("row", "col"), scatter_dimension=0, tiled=True),
        lax.psum_scatter(scale_p * factor, ("row", "col"), scatter_dimension=0, tiled=True),
    )
    (
        kernel_grad,
        bias_grad,
        gain_grad,
        shift_grad,
        win_grad,
        inb_grad,
        wout_grad,
        outb_grad,
        scale_grad,
    ) = reduced
    return (
        features_grad,
        kernel_grad,
        bias_grad,
        gain_grad,
        shift_grad,
        win_grad,
        inb_grad,
        wout_grad,
        outb_grad,
        scale_grad,
    )


def solution(mesh):
    in_specs = (
        P(None, "row", "col", None),
        P(None, "row", "col", None),
        P(None, None, ("row", "col")),
        P(("row", "col")),
        P(("row", "col")),
        P(("row", "col")),
        P(None, ("row", "col")),
        P(("row", "col")),
        P(("row", "col"), None),
        P(("row", "col")),
        P(("row", "col")),
    )
    out_specs = (
        P(None, "row", "col", None),
        P(None, None, ("row", "col")),
        P(("row", "col")),
        P(("row", "col")),
        P(("row", "col")),
        P(None, ("row", "col")),
        P(("row", "col")),
        P(("row", "col"), None),
        P(("row", "col")),
        P(("row", "col")),
    )
    return jax.shard_map(
        per_device, mesh=mesh, in_specs=in_specs, out_specs=out_specs, check_vma=False
    )
```

profile of v0, /device:TPU:1, one launch (start us, length us, event | category | flops | bytes accessed | tf_op | source)
XLA Modules:
  0.0 425.7 jit_solution(4927064167426286075)
XLA Ops:
  7.2 1.1 fusion.55
  8.4 0.8 copy.127
  9.2 7.0 %collective-permute-start = (f32[2,3,64,128]{3,0,2,1:T(2,128)}, f32[2,3,64,128]{3,0,2,1:T(2,128)}, u32[]{:S(2)}, u32[]{:S(2)}) collective-permute-start(f32[2,3,64,128]{3,0,2,1:T(2,128)} %copy.127), channel_id=1, source_target_pairs={{0,16},{16,32},{32,48},{48,64},{64,80},{80,96},{96,112},{1,17},{17... | collective-permute-start | bytes 589832 | tf_op jit(solution)/shard_map/ppermute | solution.py:17
  16.2 0.8 copy.128
  17.0 1.3 collective-permute-start.1
  18.3 38.5 %all-gather.1 = f32[128,4,128]{2,1,0:T(4,128)S(1)} all-gather(f32[1,4,128]{2,1,0:T(4,128)} %bitcast.98), channel_id=1, replica_groups=mesh['row'=8,'col'=16] {'row','col'}, dimensions={0}, use_global_device_ids=true | all-gather | bytes 264192 | tf_op jit(solution)/shard_map/all_gather | solution.py:104
  60.1 0.7 copy.73
  60.8 33.9 %all_gather.27 = f32[7,7,128]{1,0,2:T(8,128)S(1)} all-gather(f32[7,7,1]{1,0,2:T(8,128)S(1)} %copy.73), channel_id=1, replica_groups=mesh['row'=8,'col'=16] {'row','col'}, dimensions={2}, use_global_device_ids=true | all-gather | bytes 25284 | tf_op jit(solution)/shard_map/all_gather | solution.py:100
  95.2 0.8 copy.93
  97.0 63.9 %all-reduce.16 = (f32[128]{0:T(128)S(1)}, f32[128]{0:T(128)S(1)}, f32[128]{0:T(128)}, f32[512]{0:T(512)}, f32[128]{0:T(128)S(1)}, /*index=5*/f32[128]{0:T(128)}) all-reduce(f32[128]{0:T(128)S(1)} %dynamic-update-slice.3, f32[128]{0:T(128)S(1)} %dynamic-update-slice.2, ...), channel_id=1, replica_groups=mesh['row'=8,'col'=16] {'row','col'}, use_global_device_ids=true, to_apply=%add.3 | all-reduce | flops 1152 | bytes 9216
  161.1 0.9 constant_dynamic-update-slice_fusion.2
  162.1 0.9 constant_dynamic-update-slice_fusion.1
  163.0 1.0 constant_dynamic-update-slice_fusion
  164.0 1.9 collective-permute-start.2
  165.9 2.4 collective-permute-start.3
  168.3 37.6 %all-gather = f32[128,4,128]{2,1,0:T(4,128)S(1)} all-gather(f32[1,4,128]{2,1,0:T(4,128)S(1)} %bitcast.99), channel_id=1, replica_groups=mesh['row'=8,'col'=16] {'row','col'}, dimensions={0}, use_global_device_ids=true | all-gather | bytes 264192 | tf_op jit(solution)/shard_map/all_gather | solution.py:106
  206.0 0.7 fusion.51
  208.1 5.9 %fusion.56 = (f32[16,16,9]{1,2,0:T(8,128)S(1)}, f32[16,16,9,128]{3,1,2,0:T(8,128)S(1)}) fusion(f32[128]{0:T(128)S(1)} %copy-done.15, f32[7,7,1,128]{3,2,1,0:T(1,128)S(1)} %copy-done.7, f32[22,2,7,6,128]{4,2,1,3,0:T(8,128)S(1)} %slice.41, f32[22,2,8,9,128]{4,2,1,3,0:T(8,128)S(1)} %copy.72, pred[16,9]{0,1:T(8,128)(4,1)S(1)} %copy-done.16), kind=kOutput, calls=%fused_computation.87 | convolution fusion | flops 176318208 | bytes 3782800 | tf_op jit(solution)/shard_map/conv_general_dilated | solution.py:26
  214.8 0.7 multiply_reduce_fusion.2
  215.6 3.6 fusion.34
  219.2 8.0 %fusion.30 = f32[512,128]{1,0:T(8,128)} fusion(f32[2,16,64,512]{3,2,1,0:T(8,128)S(1)} %fusion.34, f32[512]{0:T(512)S(1)} %copy-done.12, f32[2,16,64,128]{3,2,1,0:T(8,128)S(1)} %copy-done.1, f32[128]{0:T(128)S(1)} %copy-done.10), kind=kOutput, calls=%fused_computation.33 | convolution fusion | flops 1616183296 | bytes 5507584 | tf_op jit(solution)/shard_map/bhwk,bhwc->kc/dot_general | solution.py:80
  227.3 5.2 %fusion.57 = (f32[512]{0:T(512)S(1)}, f32[2,16,64,512]{3,2,1,0:T(8,128)S(1)}) fusion(f32[2,16,64,512]{3,2,1,0:T(8,128)S(1)} %fusion.34, f32[512]{0:T(512)S(1)} %copy-done.12, f32[512,128,1,1]{1,0,3,2:T(8,128)S(1)} %bitcast.96, f32[2,16,64,128]{3,2,1,0:T(8,128)S(1)} %copy-done.1, f32[128]{0:T(128)S(1)} %copy-done.10), kind=kOutput, calls=%fused_computation.88 | convolution fusion | flops 1622408704 | bytes 9703936 | tf_op jit(solution)/shard_map/bhwc,kc->bhwk/dot_general | solution.py:63
  232.4 2.0 copy-done
  234.4 8.2 %fusion.28 = f32[128,512]{0,1:T(8,128)} fusion(f32[2,16,64,512]{3,2,1,0:T(8,128)S(1)} %get-tuple-element.83, f32[128]{0:T(128)S(1)} %get-tuple-element.61, f32[128]{0:T(128)S(1)} %get-tuple-element.62, f32[16,2,64,128]{3,0,2,1:T(8,128)S(1)} %slice.42, f32[2,16,64]{2,1,0:T(8,128)S(1)} %add_rsqrt_fusion, f32[2,16,64]{2,1,0:T(8,128)S(1)} %copy.79), kind=kOutput, calls=%fused_computation.31 | convolution fusion | flops 1611726848 | bytes 5522432 | tf_op jit(solution)/shard_map/bhwc,bhwk->ck/dot_general | solution.py:78
  242.7 5.7 %multiply_reduce_fusion = (f32[128]{0:T(128)S(1)}, f32[2,16,64]{2,1,0:T(8,128)S(1)}, f32[2,16,64]{2,1,0:T(8,128)S(1)}, f32[128]{0:T(128)S(1)}, f32[2,16,64,128]{3,2,1,0:T(8,128)S(1)}) fusion(f32[2,16,64]{2,1,0:T(8,128)S(1)} %add_rsqrt_fusion, f32[2,16,64]{2,1,0:T(8,128)S(1)} %copy.79, f32[16,2,64,128]{3,0,2,1:T(8,128)S(1)} %slice.42, ...), kind=kOutput, calls=%fused_computation.40 | convolution fusion | flops 1612967680 | bytes 6587904 | tf_op jit(solution)/shard_map/bhwk,ck->bhwc/dot_general | solution.py:69
  248.4 4.1 fusion.27
  252.5 1.8 fusion.52
  254.3 3.1 collective-permute-start.4
  257.5 1.7 collective-permute-start.5
  259.2 21.3 %convolution_multiply_fusion = f32[7,7,1,128]{3,2,1,0:T(1,128)S(1)} fusion(f32[2,16,64,128]{3,2,1,0:T(8,128)S(1)} %get-tuple-element.70, f32[2,22,3,128]{3,0,2,1:T(2,128)} %copy-done.6, f32[2,22,64,128]{3,0,2,1:T(2,128)} %copy-done.4, f32[2,22,3,128]{3,0,2,1:T(2,128)S(1)} %collective-permute-done.2), kind=kOutput, calls=%fused_computation.34 | convolution fusion | flops 154935424 | bytes 2650624 | tf_op jit(solution)/shard_map/transpose(jvp())/conv_general_dilated | solution.py:26
  280.8 70.8 %all-reduce.15 = (f32[7,7,128]{1,0,2:T(8,128)}, f32[128]{0:T(128)S(1)}, f32[128]{0:T(128)S(1)}, f32[128]{0:T(128)S(1)}, f32[512]{0:T(512)S(1)}, /*index=5*/f32[128]{0:T(128)S(1)}, f32[128]{0:T(128)S(1)}) all-reduce(f32[7,7,128]{1,0,2:T(8,128)S(1)} %bitcast.94, ...), channel_id=2, replica_groups=mesh['row'=8,'col'=16] {'row','col'}, use_global_device_ids=true, to_apply=%region_4.0.clone | all-reduce | flops 7424 | bytes 59392
  351.6 0.6 dynamic-slice.8
  352.2 0.6 dynamic-slice.7
  352.8 0.6 dynamic-slice.3
  353.4 0.6 dynamic-slice.2
  354.0 0.6 dynamic-slice.1
  354.6 0.7 constant_dynamic-slice_fusion.2
  355.2 0.6 copy.88
  356.5 2.4 collective-permute-start.6
  358.9 2.1 collective-permute-start.7
  361.0 44.3 %all-reduce.20.cloned.1.call-done = (f32[128,512]{0,1:T(8,128)}, f32[512,128]{1,0:T(8,128)}) async-done(((f32[128,512]{0,1:T(8,128)}, f32[512,128]{1,0:T(8,128)}), (f32[128,512]{0,1:T(8,128)}, f32[512,128]{1,0:T(8,128)})) %all-reduce.20.cloned.1.call-update) | async-done | bytes 524304
  405.3 1.3 constant_dynamic-slice_fusion.1
  406.6 1.3 constant_dynamic-slice_fusion
  408.0 0.8 copy.96
  409.8 1.0 fusion.5
  410.8 5.4 %fusion.18 = f32[16,16,9,128]{3,1,2,0:T(8,128)S(1)} fusion(f32[7,7,1,128]{3,2,1,0:T(1,128)S(1)} %copy.82, f32[22,2,8,15,128]{4,1,3,2,0:T(2,128)S(1)} %fusion.5, pred[16,9]{0,1:T(8,128)(4,1)S(1)} %copy-done.17), kind=kOutput, calls=%fused_computation.26 | convolution fusion | flops 173703168 | bytes 3908240 | tf_op jit(solution)/shard_map/conv_general_dilated | solution.py:26
  416.7 0.6 fusion.31
  417.3 1.3 copy.87
  (85 shorter events, 6.3 us)
Async XLA Ops:
  7.2 89.5 %copy-start.13 = (f32[4]{0:T(128)S(1)}, f32[4]{0:T(128)}, u32[]{:S(2)}) copy-start(f32[4]{0:T(128)} %param.18) | copy-start | bytes 52
  7.2 153.6 %copy-start.1 = (f32[2,16,64,128]{3,2,1,0:T(8,128)S(1)}, f32[2,16,64,128]{3,2,1,0:T(8,128)}, u32[]{:S(2)}) copy-start(f32[2,16,64,128]{3,2,1,0:T(8,128)} %param.12) | copy-start | bytes 3145732
  7.2 398.1 %all-reduce.20.cloned.1.call-start = ((), (), s32[]{:S(2)}) async-start(), calls=%async_computation | async-start | bytes 1048576
  8.4 153.7 %copy-start.5 = (f32[2,16,64,128]{3,2,1,0:T(8,128)S(1)}, f32[2,16,64,128]{3,2,1,0:T(8,128)}, u32[]{:S(2)}) copy-start(f32[2,16,64,128]{3,2,1,0:T(8,128)} %param.11) | copy-start | bytes 3145732
  9.2 151.9 %collective-permute-start = (f32[2,3,64,128]{3,0,2,1:T(2,128)}, f32[2,3,64,128]{3,0,2,1:T(2,128)}, u32[]{:S(2)}, u32[]{:S(2)}) collective-permute-start(f32[2,3,64,128]{3,0,2,1:T(2,128)} %copy.127), channel_id=1, source_target_pairs={{0,16},{16,32},{32,48},{48,64},{64,80},{80,96},{96,112},{1,17},{17... | collective-permute-start | bytes 589832 | tf_op jit(solution)/shard_map/ppermute | solution.py:17
  17.0 145.9 %collective-permute-start.1 = (f32[2,3,64,128]{3,0,2,1:T(2,128)}, f32[2,3,64,128]{3,0,2,1:T(2,128)}, u32[]{:S(2)}, u32[]{:S(2)}) collective-permute-start(f32[2,3,64,128]{3,0,2,1:T(2,128)} %copy.128), channel_id=1, source_target_pairs={{16,0},{32,16},{48,32},{64,48},{80,64},{96,80},{112,96},{17,1},{33... | collective-permute-start | bytes 589832 | tf_op jit(solution)/shard_map/ppermute | solution.py:20
  95.2 73.2 %copy-start.8 = (f32[4,128]{1,0:T(4,128)S(1)}, f32[4,128]{1,0:T(4,128)}, u32[]{:S(2)}) copy-start(f32[4,128]{1,0:T(4,128)} %param.19) | copy-start | bytes 6148
  160.8 7.5 %copy-start.9 = (f32[128]{0:T(128)}, f32[128]{0:T(128)S(1)}, u32[]{:S(2)}) copy-start(f32[128]{0:T(128)S(1)} %get-tuple-element.65) | copy-start | bytes 1540
  163.9 43.4 %copy-start.4 = (f32[2,22,64,128]{3,0,2,1:T(2,128)}, f32[2,22,64,128]{3,0,2,1:T(2,128)S(1)}, u32[]{:S(2)}) copy-start(f32[2,22,64,128]{3,0,2,1:T(2,128)S(1)} %constant_dynamic-update-slice_fusion) | copy-start | bytes 4325380
  164.0 42.0 %collective-permute-start.2 = (f32[2,22,3,128]{3,0,2,1:T(2,128)S(1)}, f32[2,22,3,128]{3,0,2,1:T(2,128)S(1)}, u32[]{:S(2)}, u32[]{:S(2)}) collective-permute-start(f32[2,22,3,128]{3,0,2,1:T(2,128)S(1)} %get-tuple-element.73), channel_id=1, source_target_pairs={{0,1},{1,2},{2,3},{3,4},{4,5},{5,6},{6,7},{7,8},{8,9},{9,10},{10,1... | collective-permute-start | bytes 202760 | tf_op jit(solution)/shard_map/ppermute | solution.py:17
  165.9 40.1 %collective-permute-start.3 = (f32[2,22,3,128]{3,0,2,1:T(2,128)S(1)}, f32[2,22,3,128]{3,0,2,1:T(2,128)S(1)}, u32[]{:S(2)}, u32[]{:S(2)}) collective-permute-start(f32[2,22,3,128]{3,0,2,1:T(2,128)S(1)} %get-tuple-element.74), channel_id=1, source_target_pairs={{1,0},{2,1},{3,2},{4,3},{5,4},{6,5},{7,6},{8,7},{9,8},{10,9},{11,1... | collective-permute-start | bytes 202760 | tf_op jit(solution)/shard_map/ppermute | solution.py:20
  206.0 1.6 copy-start.6
  207.3 0.7 copy-start.7
  207.3 0.7 copy-start.15
  207.3 0.7 copy-start.16
  215.5 3.7 copy-start.10
  215.5 3.7 copy-start.12
  219.2 8.1 %copy-start.2 = (f32[2,16,64,512]{3,2,1,0:T(8,128)}, f32[2,16,64,512]{3,2,1,0:T(8,128)S(1)}, u32[]{:S(2)}) copy-start(f32[2,16,64,512]{3,2,1,0:T(8,128)S(1)} %fusion.34) | copy-start | bytes 12582916
  232.4 2.0 copy-start
  242.7 5.7 %copy-start.3 = (f32[2,16,64,512]{3,2,1,0:T(8,128)S(1)}, f32[2,16,64,512]{3,2,1,0:T(8,128)}, u32[]{:S(2)}) copy-start(f32[2,16,64,512]{3,2,1,0:T(8,128)} %copy-done.2) | copy-start | bytes 12582916
  242.7 5.7 %copy-start.14 = (f32[128]{0:T(128)S(1)}, f32[128]{0:T(128)}, u32[]{:S(2)}) copy-start(f32[128]{0:T(128)} %get-tuple-element.66) | copy-start | bytes 1540
  254.3 102.1 %collective-permute-start.4 = (f32[2,3,64,128]{3,2,1,0:T(8,128)S(1)}, f32[2,3,64,128]{3,2,1,0:T(8,128)S(1)}, u32[]{:S(2)}, u32[]{:S(2)}) collective-permute-start(f32[2,3,64,128]{3,2,1,0:T(8,128)S(1)} %get-tuple-element.75), channel_id=1, source_target_pairs={{0,16},{16,32},{32,48},{48,64},{64,80},{80,96},{96,112},{1,17},{17... | collective-permute-start | bytes 589832 | tf_op jit(solution)/shard_map/ppermute | solution.py:17
  257.5 99.0 %collective-permute-start.5 = (f32[2,3,64,128]{3,2,1,0:T(8,128)S(1)}, f32[2,3,64,128]{3,2,1,0:T(8,128)S(1)}, u32[]{:S(2)}, u32[]{:S(2)}) collective-permute-start(f32[2,3,64,128]{3,2,1,0:T(8,128)S(1)} %get-tuple-element.76), channel_id=1, source_target_pairs={{16,0},{32,16},{48,32},{64,48},{80,64},{96,80},{112,96},{17,1},{33... | collective-permute-start | bytes 589832 | tf_op jit(solution)/shard_map/ppermute | solution.py:20
  259.2 21.3 %copy-start.11 = (f32[128]{0:T(128)S(1)}, f32[128]{0:T(128)}, u32[]{:S(2)}) copy-start(f32[128]{0:T(128)} %get-tuple-element.69) | copy-start | bytes 1540
  356.5 51.4 %collective-permute-start.6 = (f32[2,22,3,128]{3,2,1,0:T(4,128)S(1)}, f32[2,22,3,128]{3,2,1,0:T(4,128)S(1)}, u32[]{:S(2)}, u32[]{:S(2)}) collective-permute-start(f32[2,22,3,128]{3,2,1,0:T(4,128)S(1)} %get-tuple-element.71), channel_id=1, source_target_pairs={{0,1},{1,2},{2,3},{3,4},{4,5},{5,6},{6,7},{7,8},{8,9},{9,10},{10,1... | collective-permute-start | bytes 202760 | tf_op jit(solution)/shard_map/ppermute | solution.py:17
  358.9 48.9 %collective-permute-start.7 = (f32[2,22,3,128]{3,2,1,0:T(4,128)S(1)}, f32[2,22,3,128]{3,2,1,0:T(4,128)S(1)}, u32[]{:S(2)}, u32[]{:S(2)}) collective-permute-start(f32[2,22,3,128]{3,2,1,0:T(4,128)S(1)} %get-tuple-element.72), channel_id=1, source_target_pairs={{1,0},{2,1},{3,2},{4,3},{5,4},{6,5},{7,6},{8,7},{9,8},{10,9},{11,1... | collective-permute-start | bytes 202760 | tf_op jit(solution)/shard_map/ppermute | solution.py:20
  409.8 1.1 copy-start.17
Sparse Core Ops, SparseCore 0:
  259.3 145.9 all-reduce.19
where the time goes:
time: 432 us; the launch traced here: 426 us
  blocking collectives  245 us (57%)
  matrix products  67.6 us (16%)
  waiting for transfers between devices  44.3 us (10%)
  local copies, waits for them, and re-layouts  23.5 us (5%)
  starting transfers between devices  22 us (5%)
  between operations  18.1 us (4%)
  other arithmetic  5.48 us (1%)
    unnamed x2, blocking collectives  135 us
    unnamed x2, waiting for transfers between devices  44.3 us
    all_gather x1, blocking collectives, per_device(): lax.all_gather(w_in, ('row', 'col'), axis=1, tiled=True)  38.5 us
    all_gather x1, blocking collectives, per_device(): lax.all_gather(w_out, ('row', 'col'), axis=0, tiled=True)  37.6 us
    all_gather x1, blocking collectives, per_device(): lax.all_gather(conv_kernel, ('row', 'col'), axis=2, tiled=True)  33.9 us
    conv_general_dilated x3, matrix products, depthwise(): lax.conv_general_dilated(field, kernel[:, :, None, :], (1, 1), 'VALID', d...  32.7 us
    unnamed x65, local copies, waits for them, and re-layouts  16.8 us
    ppermute x4, starting transfers between devices, extended(): lax.ppermute(lax.slice_in_dim(block, block.shape[dim] - width, None, axis...  14.4 us
  transfers between devices with their start and end apart: 9, of which 1 were waited for; matrix products, arithmetic and copies ran while one was open for 8% of the time, Pallas kernels for 0%

commit v1 on v0

--- a/solution.py
+++ b/solution.py
@@ -101,7 +101,10 @@
         lax.all_gather(conv_bias, ("row", "col"), axis=0, tiled=True),
         lax.all_gather(norm_gain, ("row", "col"), axis=0, tiled=True),
         lax.all_gather(norm_shift, ("row", "col"), axis=0, tiled=True),
-        lax.all_gather(w_in, ("row", "col"), axis=1, tiled=True),
+        jnp.concatenate(
+            lax.all_to_all(jnp.stack([w_in] * lax.axis_size(("row", "col"))), ("row", "col"), 0, 0),
+            axis=1,
+        ),
         lax.all_gather(in_bias, ("row", "col"), axis=0, tiled=True),
         lax.all_gather(w_out, ("row", "col"), axis=0, tiled=True),
         lax.all_gather(out_bias, ("row", "col"), axis=0, tiled=True),

time: 432 us -> 409 us (0.947)
  blocking collectives: 245 us -> 212 us
  starting transfers between devices: 22 us -> 30.4 us
    all_gather x1 -> x0, blocking collectives: 38.5 us -> none  [per_device(): lax.all_gather(w_in, ('row', 'col'), axis=1, tiled=True)]
    all_to_all x0 -> x1, starting transfers between devices: none -> 7.68 us  [per_device(): lax.all_to_all(jnp.stack([w_in] * lax.axis_size(('row', 'col'))), ('row',...]
    all_gather x1, blocking collectives: 33.9 us -> 40.9 us  [per_device(): lax.all_gather(conv_kernel, ('row', 'col'), axis=2, tiled=True)]
  transfers between devices with their start and end apart: 9 -> 10, of which waited for: 1 -> 1; matrix products, arithmetic and copies ran while one was open for 8% -> 11% of each run, Pallas kernels for 0% -> 0%
where the time goes in v1:
time: 409 us; the launch traced here: 403 us
  blocking collectives  212 us (52%)
  matrix products  67.6 us (17%)
  waiting for transfers between devices  44.7 us (11%)
  starting transfers between devices  30.4 us (7%)
  local copies, waits for them, and re-layouts  24.9 us (6%)
  between operations  18.1 us (4%)
  other arithmetic  5.48 us (1%)
    unnamed x2, blocking collectives  134 us
    unnamed x2, waiting for transfers between devices  44.7 us
    all_gather x1, blocking collectives, per_device(): lax.all_gather(conv_kernel, ('row', 'col'), axis=2, tiled=True)  40.9 us
    all_gather x1, blocking collectives, per_device(): lax.all_gather(w_out, ('row', 'col'), axis=0, tiled=True)  37 us
    conv_general_dilated x3, matrix products, depthwise(): lax.conv_general_dilated(field, kernel[:, :, None, :], (1, 1), 'VALID', d...  32.7 us
    unnamed x65, local copies, waits for them, and re-layouts  16.8 us
    ppermute x4, starting transfers between devices, extended(): lax.ppermute(lax.slice_in_dim(block, block.shape[dim] - width, None, axis...  15.2 us
    dot_general x1, matrix products, mixing_back(): win_grad = jnp.einsum('bhwc,bhwk->ck', lin, d_act, precision=highest)  8.25 us
  transfers between devices with their start and end apart: 10, of which 1 were waited for; matrix products, arithmetic and copies ran while one was open for 11% of the time, Pallas kernels for 0%

profile of v1, /device:TPU:1, one launch (start us, length us, event | category | flops | bytes accessed | tf_op | source)
XLA Modules:
  0.0 402.9 jit_solution(15342003411575332542)
XLA Ops:
  7.2 1.1 fusion.55
  8.3 0.8 copy.137
  9.2 7.1 %collective-permute-start = (f32[2,3,64,128]{3,0,2,1:T(2,128)}, f32[2,3,64,128]{3,0,2,1:T(2,128)}, u32[]{:S(2)}, u32[]{:S(2)}) collective-permute-start(f32[2,3,64,128]{3,0,2,1:T(2,128)} %copy.137), channel_id=1, source_target_pairs={{0,16},{16,32},{32,48},{48,64},{64,80},{80,96},{96,112},{1,17},{17... | collective-permute-start | bytes 589832 | tf_op jit(solution)/shard_map/ppermute | solution.py:17
  16.3 1.4 stack.2
  17.7 7.7 %all-to-all-start = ((f32[128,128,4]{1,2,0:T(4,128)}), f32[128,128,4]{1,2,0:T(4,128)S(1)}, u32[]{:S(2)}, u32[]{:S(2)}) async-start(f32[128,128,4]{1,2,0:T(4,128)} %stack.2), calls=%async_computation | async-start | bytes 524288 | tf_op jit(solution)/shard_map/all_to_all | solution.py:105
  25.4 0.8 copy.138
  26.3 1.3 collective-permute-start.1
  30.8 0.7 copy.78
  31.5 40.9 %all_gather.24 = f32[7,7,128]{1,0,2:T(8,128)S(1)} all-gather(f32[7,7,1]{1,0,2:T(8,128)S(1)} %copy.78), channel_id=1, replica_groups=mesh['row'=8,'col'=16] {'row','col'}, dimensions={2}, use_global_device_ids=true | all-gather | bytes 25284 | tf_op jit(solution)/shard_map/all_gather | solution.py:100
  72.8 0.8 copy.101
  74.6 62.8 %all-reduce.16 = (f32[128]{0:T(128)S(1)}, f32[128]{0:T(128)S(1)}, f32[128]{0:T(128)}, f32[512]{0:T(512)}, f32[128]{0:T(128)S(1)}, /*index=5*/f32[128]{0:T(128)}) all-reduce(f32[128]{0:T(128)S(1)} %dynamic-update-slice.3, f32[128]{0:T(128)S(1)} %dynamic-update-slice.2, ...), channel_id=1, replica_groups=mesh['row'=8,'col'=16] {'row','col'}, use_global_device_ids=true, to_apply=%add.3 | all-reduce | flops 1152 | bytes 9216
  137.7 0.9 constant_dynamic-update-slice_fusion.2
  138.7 0.9 constant_dynamic-update-slice_fusion.1
  139.6 1.0 constant_dynamic-update-slice_fusion
  140.6 3.0 collective-permute-start.2
  143.6 1.9 collective-permute-start.3
  145.5 37.0 %all-gather = f32[128,4,128]{2,1,0:T(4,128)S(1)} all-gather(f32[1,4,128]{2,1,0:T(4,128)S(1)} %bitcast.96), channel_id=1, replica_groups=mesh['row'=8,'col'=16] {'row','col'}, dimensions={0}, use_global_device_ids=true | all-gather | bytes 264192 | tf_op jit(solution)/shard_map/all_gather | solution.py:109
  182.6 0.7 fusion.51
  184.7 5.9 %fusion.56 = (f32[16,16,9]{1,2,0:T(8,128)S(1)}, f32[16,16,9,128]{3,1,2,0:T(8,128)S(1)}) fusion(f32[128]{0:T(128)S(1)} %copy-done.15, f32[7,7,1,128]{3,2,1,0:T(1,128)S(1)} %copy-done.7, f32[22,2,7,6,128]{4,2,1,3,0:T(8,128)S(1)} %slice.41, f32[22,2,8,9,128]{4,2,1,3,0:T(8,128)S(1)} %copy.77, pred[16,9]{0,1:T(8,128)(4,1)S(1)} %copy-done.16), kind=kOutput, calls=%fused_computation.87 | convolution fusion | flops 176318208 | bytes 3782800 | tf_op jit(solution)/shard_map/conv_general_dilated | solution.py:26
  191.4 0.7 multiply_reduce_fusion.2
  192.2 3.6 fusion.34
  195.8 8.0 %fusion.30 = f32[512,128]{1,0:T(8,128)} fusion(f32[2,16,64,512]{3,2,1,0:T(8,128)S(1)} %fusion.34, f32[512]{0:T(512)S(1)} %copy-done.12, f32[2,16,64,128]{3,2,1,0:T(8,128)S(1)} %copy-done.1, f32[128]{0:T(128)S(1)} %copy-done.10), kind=kOutput, calls=%fused_computation.33 | convolution fusion | flops 1616183296 | bytes 5507584 | tf_op jit(solution)/shard_map/bhwk,bhwc->kc/dot_general | solution.py:80
  203.9 5.2 %fusion.57 = (f32[512]{0:T(512)S(1)}, f32[2,16,64,512]{3,2,1,0:T(8,128)S(1)}) fusion(f32[2,16,64,512]{3,2,1,0:T(8,128)S(1)} %fusion.34, f32[512]{0:T(512)S(1)} %copy-done.12, f32[512,128,1,1]{1,0,3,2:T(8,128)S(1)} %bitcast.94, f32[2,16,64,128]{3,2,1,0:T(8,128)S(1)} %copy-done.1, f32[128]{0:T(128)S(1)} %copy-done.10), kind=kOutput, calls=%fused_computation.88 | convolution fusion | flops 1622408704 | bytes 9703936 | tf_op jit(solution)/shard_map/bhwc,kc->bhwk/dot_general | solution.py:63
  209.1 2.0 copy-done
  211.0 8.3 %fusion.28 = f32[128,512]{0,1:T(8,128)} fusion(f32[2,16,64,512]{3,2,1,0:T(8,128)S(1)} %get-tuple-element.83, f32[128]{0:T(128)S(1)} %get-tuple-element.61, f32[128]{0:T(128)S(1)} %get-tuple-element.62, f32[16,2,64,128]{3,0,2,1:T(8,128)S(1)} %slice.42, f32[2,16,64]{2,1,0:T(8,128)S(1)} %add_rsqrt_fusion, f32[2,16,64]{2,1,0:T(8,128)S(1)} %copy.84), kind=kOutput, calls=%fused_computation.31 | convolution fusion | flops 1611726848 | bytes 5522432 | tf_op jit(solution)/shard_map/bhwc,bhwk->ck/dot_general | solution.py:78
  219.3 5.7 %multiply_reduce_fusion = (f32[128]{0:T(128)S(1)}, f32[2,16,64]{2,1,0:T(8,128)S(1)}, f32[2,16,64]{2,1,0:T(8,128)S(1)}, f32[128]{0:T(128)S(1)}, f32[2,16,64,128]{3,2,1,0:T(8,128)S(1)}) fusion(f32[2,16,64]{2,1,0:T(8,128)S(1)} %add_rsqrt_fusion, f32[2,16,64]{2,1,0:T(8,128)S(1)} %copy.84, f32[16,2,64,128]{3,0,2,1:T(8,128)S(1)} %slice.42, ...), kind=kOutput, calls=%fused_computation.40 | convolution fusion | flops 1612967680 | bytes 6587904 | tf_op jit(solution)/shard_map/bhwk,ck->bhwc/dot_general | solution.py:69
  225.0 4.1 %fusion.27 = f32[128]{0:T(128)S(1)} fusion(f32[2,16,64,128]{3,2,1,0:T(8,128)S(1)} %copy-done.1, f32[512,128,1,1]{1,0,3,2:T(8,128)S(1)} %bitcast.95, f32[2,16,64,512]{3,2,1,0:T(8,128)S(1)} %copy-done.3, f32[512]{0:T(512)S(1)} %copy-done.12, f32[128]{0:T(128)S(1)} %copy-done.14), kind=kOutput, calls=%fused_computation.29 | convolution fusion | flops 1616641920 | bytes 5508096 | tf_op jit(solution)/shard_map/bhwk,kc->bhwc/dot_general | solution.py:61
  229.1 1.8 fusion.52
  231.0 3.1 collective-permute-start.4
  234.1 1.7 collective-permute-start.5
  235.9 21.3 %convolution_multiply_fusion = f32[7,7,1,128]{3,2,1,0:T(1,128)S(1)} fusion(f32[2,16,64,128]{3,2,1,0:T(8,128)S(1)} %get-tuple-element.70, f32[2,22,3,128]{3,0,2,1:T(2,128)} %copy-done.6, f32[2,22,64,128]{3,0,2,1:T(2,128)} %copy-done.4, f32[2,22,3,128]{3,0,2,1:T(2,128)S(1)} %collective-permute-done.2), kind=kOutput, calls=%fused_computation.34 | convolution fusion | flops 154935424 | bytes 2650624 | tf_op jit(solution)/shard_map/transpose(jvp())/conv_general_dilated | solution.py:26
  257.5 71.0 %all-reduce.15 = (f32[7,7,128]{1,0,2:T(8,128)}, f32[128]{0:T(128)S(1)}, f32[128]{0:T(128)S(1)}, f32[128]{0:T(128)S(1)}, f32[512]{0:T(512)S(1)}, /*index=5*/f32[128]{0:T(128)S(1)}, f32[128]{0:T(128)S(1)}) all-reduce(f32[7,7,128]{1,0,2:T(8,128)S(1)} %bitcast.92, ...), channel_id=2, replica_groups=mesh['row'=8,'col'=16] {'row','col'}, use_global_device_ids=true, to_apply=%region_4.0.clone | all-reduce | flops 7424 | bytes 59392
  328.5 0.6 dynamic-slice.8
  329.1 0.6 dynamic-slice.7
  329.6 0.6 dynamic-slice.3
  330.8 0.6 dynamic-slice.1
  331.4 0.7 constant_dynamic-slice_fusion.2
  332.1 0.6 copy.95
  333.3 2.0 collective-permute-start.6
  335.3 2.6 collective-permute-start.7
  337.8 44.7 %all-reduce.20.cloned.1.call-done = (f32[128,512]{0,1:T(8,128)}, f32[512,128]{1,0:T(8,128)}) async-done(((f32[128,512]{0,1:T(8,128)}, f32[512,128]{1,0:T(8,128)}), (f32[128,512]{0,1:T(8,128)}, f32[512,128]{1,0:T(8,128)})) %all-reduce.20.cloned.1.call-update) | async-done | bytes 524304
  382.5 1.3 constant_dynamic-slice_fusion.1
  383.8 1.3 constant_dynamic-slice_fusion
  385.2 0.8 copy.106
  387.0 1.0 fusion.5
  388.0 5.4 %fusion.18 = f32[16,16,9,128]{3,1,2,0:T(8,128)S(1)} fusion(f32[7,7,1,128]{3,2,1,0:T(1,128)S(1)} %copy.89, f32[22,2,8,15,128]{4,1,3,2,0:T(2,128)S(1)} %fusion.5, pred[16,9]{0,1:T(8,128)(4,1)S(1)} %copy-done.17), kind=kOutput, calls=%fused_computation.26 | convolution fusion | flops 173703168 | bytes 3908240 | tf_op jit(solution)/shard_map/conv_general_dilated | solution.py:26
  393.9 0.6 fusion.31
  394.5 1.3 copy.94
  (87 shorter events, 6.9 us)
Async XLA Ops:
  7.2 67.2 %copy-start.13 = (f32[4]{0:T(128)S(1)}, f32[4]{0:T(128)}, u32[]{:S(2)}) copy-start(f32[4]{0:T(128)} %param.18) | copy-start | bytes 52
  7.2 130.2 %copy-start.1 = (f32[2,16,64,128]{3,2,1,0:T(8,128)S(1)}, f32[2,16,64,128]{3,2,1,0:T(8,128)}, u32[]{:S(2)}) copy-start(f32[2,16,64,128]{3,2,1,0:T(8,128)} %param.12) | copy-start | bytes 3145732
  9.2 129.5 %copy-start.5 = (f32[2,16,64,128]{3,2,1,0:T(8,128)S(1)}, f32[2,16,64,128]{3,2,1,0:T(8,128)}, u32[]{:S(2)}) copy-start(f32[2,16,64,128]{3,2,1,0:T(8,128)} %param.11) | copy-start | bytes 3145732
  9.2 128.5 %collective-permute-start = (f32[2,3,64,128]{3,0,2,1:T(2,128)}, f32[2,3,64,128]{3,0,2,1:T(2,128)}, u32[]{:S(2)}, u32[]{:S(2)}) collective-permute-start(f32[2,3,64,128]{3,0,2,1:T(2,128)} %copy.137), channel_id=1, source_target_pairs={{0,16},{16,32},{32,48},{48,64},{64,80},{80,96},{96,112},{1,17},{17... | collective-permute-start | bytes 589832 | tf_op jit(solution)/shard_map/ppermute | solution.py:17
  17.7 174.4 %all-to-all-start = ((f32[128,128,4]{1,2,0:T(4,128)}), f32[128,128,4]{1,2,0:T(4,128)S(1)}, u32[]{:S(2)}, u32[]{:S(2)}) async-start(f32[128,128,4]{1,2,0:T(4,128)} %stack.2), calls=%async_computation | async-start | bytes 524288 | tf_op jit(solution)/shard_map/all_to_all | solution.py:105
  25.4 357.1 %all-reduce.20.cloned.1.call-start = ((), (), s32[]{:S(2)}) async-start(), calls=%async_computation.1 | async-start | bytes 1048576
  26.3 113.3 %collective-permute-start.1 = (f32[2,3,64,128]{3,0,2,1:T(2,128)}, f32[2,3,64,128]{3,0,2,1:T(2,128)}, u32[]{:S(2)}, u32[]{:S(2)}) collective-permute-start(f32[2,3,64,128]{3,0,2,1:T(2,128)} %copy.138), channel_id=1, source_target_pairs={{16,0},{32,16},{48,32},{64,48},{80,64},{96,80},{112,96},{17,1},{33... | collective-permute-start | bytes 589832 | tf_op jit(solution)/shard_map/ppermute | solution.py:20
  72.8 72.7 %copy-start.8 = (f32[4,128]{1,0:T(4,128)S(1)}, f32[4,128]{1,0:T(4,128)}, u32[]{:S(2)}) copy-start(f32[4,128]{1,0:T(4,128)} %param.19) | copy-start | bytes 6148
  137.4 8.1 %copy-start.9 = (f32[128]{0:T(128)}, f32[128]{0:T(128)S(1)}, u32[]{:S(2)}) copy-start(f32[128]{0:T(128)S(1)} %get-tuple-element.65) | copy-start | bytes 1540
  140.5 43.4 %copy-start.4 = (f32[2,22,64,128]{3,0,2,1:T(2,128)}, f32[2,22,64,128]{3,0,2,1:T(2,128)S(1)}, u32[]{:S(2)}) copy-start(f32[2,22,64,128]{3,0,2,1:T(2,128)S(1)} %constant_dynamic-update-slice_fusion) | copy-start | bytes 4325380
  140.6 42.0 %collective-permute-start.2 = (f32[2,22,3,128]{3,0,2,1:T(2,128)S(1)}, f32[2,22,3,128]{3,0,2,1:T(2,128)S(1)}, u32[]{:S(2)}, u32[]{:S(2)}) collective-permute-start(f32[2,22,3,128]{3,0,2,1:T(2,128)S(1)} %get-tuple-element.73), channel_id=1, source_target_pairs={{0,1},{1,2},{2,3},{3,4},{4,5},{5,6},{6,7},{7,8},{8,9},{9,10},{10,1... | collective-permute-start | bytes 202760 | tf_op jit(solution)/shard_map/ppermute | solution.py:17
  143.6 39.0 %collective-permute-start.3 = (f32[2,22,3,128]{3,0,2,1:T(2,128)S(1)}, f32[2,22,3,128]{3,0,2,1:T(2,128)S(1)}, u32[]{:S(2)}, u32[]{:S(2)}) collective-permute-start(f32[2,22,3,128]{3,0,2,1:T(2,128)S(1)} %get-tuple-element.74), channel_id=1, source_target_pairs={{1,0},{2,1},{3,2},{4,3},{5,4},{6,5},{7,6},{8,7},{9,8},{10,9},{11,1... | collective-permute-start | bytes 202760 | tf_op jit(solution)/shard_map/ppermute | solution.py:20
  182.6 1.6 copy-start.6
  183.9 0.7 copy-start.7
  183.9 0.7 copy-start.15
  183.9 0.7 copy-start.16
  192.1 3.7 copy-start.10
  192.1 3.7 copy-start.12
  195.8 8.1 %copy-start.2 = (f32[2,16,64,512]{3,2,1,0:T(8,128)}, f32[2,16,64,512]{3,2,1,0:T(8,128)S(1)}, u32[]{:S(2)}) copy-start(f32[2,16,64,512]{3,2,1,0:T(8,128)S(1)} %fusion.34) | copy-start | bytes 12582916
  209.0 2.0 copy-start
  219.3 5.7 %copy-start.3 = (f32[2,16,64,512]{3,2,1,0:T(8,128)S(1)}, f32[2,16,64,512]{3,2,1,0:T(8,128)}, u32[]{:S(2)}) copy-start(f32[2,16,64,512]{3,2,1,0:T(8,128)} %copy-done.2) | copy-start | bytes 12582916
  219.3 5.7 %copy-start.14 = (f32[128]{0:T(128)S(1)}, f32[128]{0:T(128)}, u32[]{:S(2)}) copy-start(f32[128]{0:T(128)} %get-tuple-element.66) | copy-start | bytes 1540
  231.0 102.3 %collective-permute-start.4 = (f32[2,3,64,128]{3,2,1,0:T(8,128)S(1)}, f32[2,3,64,128]{3,2,1,0:T(8,128)S(1)}, u32[]{:S(2)}, u32[]{:S(2)}) collective-permute-start(f32[2,3,64,128]{3,2,1,0:T(8,128)S(1)} %get-tuple-element.75), channel_id=1, source_target_pairs={{0,16},{16,32},{32,48},{48,64},{64,80},{80,96},{96,112},{1,17},{17... | collective-permute-start | bytes 589832 | tf_op jit(solution)/shard_map/ppermute | solution.py:17
  234.1 99.1 %collective-permute-start.5 = (f32[2,3,64,128]{3,2,1,0:T(8,128)S(1)}, f32[2,3,64,128]{3,2,1,0:T(8,128)S(1)}, u32[]{:S(2)}, u32[]{:S(2)}) collective-permute-start(f32[2,3,64,128]{3,2,1,0:T(8,128)S(1)} %get-tuple-element.76), channel_id=1, source_target_pairs={{16,0},{32,16},{48,32},{64,48},{80,64},{96,80},{112,96},{17,1},{33... | collective-permute-start | bytes 589832 | tf_op jit(solution)/shard_map/ppermute | solution.py:20
  235.9 21.3 %copy-start.11 = (f32[128]{0:T(128)S(1)}, f32[128]{0:T(128)}, u32[]{:S(2)}) copy-start(f32[128]{0:T(128)} %get-tuple-element.69) | copy-start | bytes 1540
  333.3 51.7 %collective-permute-start.6 = (f32[2,22,3,128]{3,2,1,0:T(4,128)S(1)}, f32[2,22,3,128]{3,2,1,0:T(4,128)S(1)}, u32[]{:S(2)}, u32[]{:S(2)}) collective-permute-start(f32[2,22,3,128]{3,2,1,0:T(4,128)S(1)} %get-tuple-element.71), channel_id=1, source_target_pairs={{0,1},{1,2},{2,3},{3,4},{4,5},{5,6},{6,7},{7,8},{8,9},{9,10},{10,1... | collective-permute-start | bytes 202760 | tf_op jit(solution)/shard_map/ppermute | solution.py:17
  335.3 49.8 %collective-permute-start.7 = (f32[2,22,3,128]{3,2,1,0:T(4,128)S(1)}, f32[2,22,3,128]{3,2,1,0:T(4,128)S(1)}, u32[]{:S(2)}, u32[]{:S(2)}) collective-permute-start(f32[2,22,3,128]{3,2,1,0:T(4,128)S(1)} %get-tuple-element.72), channel_id=1, source_target_pairs={{1,0},{2,1},{3,2},{4,3},{5,4},{6,5},{7,6},{8,7},{9,8},{10,9},{11,1... | collective-permute-start | bytes 202760 | tf_op jit(solution)/shard_map/ppermute | solution.py:20
  387.0 1.1 copy-start.17
Sparse Core Ops, SparseCore 0:
  236.0 146.4 all-reduce.19
